TPU v7x, 256 devices: a whole 4x4x8 slice. The times are simulated.
256 devices in a mesh: expert: 8 (over x, core), latent: 32 (over y, z).
Axes of the slice: x: 4, y: 4, z: 8, core: 2. Of those that a mesh axis runs over, the one named last changes fastest.
Arguments:
- tokens: bfloat16 [2048, 2560], P(('expert', 'latent')), may hold values from -6 to 6
- route: int32 [2048, 1], P(('expert', 'latent')), may hold values from 0 to 7; in each aligned block of 8 rows (0 to 7, 8 to 15, ...) at most 2 rows name the same one
- blocks: int32 [2048, 64], P(('expert', 'latent')), may hold values from 0 to 255, all different within a row
- weight: bfloat16 [8, 2560, 32768], P('expert', None, 'latent'), may hold values from -0.125 to 0.125
- enc_bias: float32 [8, 32768], P('expert', 'latent'), may hold values from -3 to 3
- dec_bias: float32 [2560], replicated, may hold values from -3 to 3
Outputs:
- grad_weight: bfloat16 [8, 2560, 32768], P('expert', None, 'latent')
- grad_enc: float32 [8, 32768], P('expert', 'latent')
- grad_dec: float32 [2560], replicated
- loss: float32 [], replicated
Inputs may be any that keep to these rules, and one draw needn't show every extreme that they name: `route`: within the rows of one device (aligned blocks of 8 rows) no expert is named by more than 2 rows. Each row lists 64 different blocks.
All inputs are finite; a program needn't handle non-finite values.
Results may differ from a plain program's by a relative error of at most 0.012.
The roundings to bfloat16 on the way count: a program that leaves them out, or rounds other values in their place, can miss the bound.
Values may be sent and summed in bfloat16 or wider, within the bound.
No kernel may reach another device: no remote copies, remote signals or barrier semaphores. Data moves between devices by JAX's collectives and lax.ppermute only.
A program may use at most 128 MiB of HBM per device.

v0:
```python
import jax
import jax.numpy as jnp
from jax import lax
from jax.sharding import PartitionSpec as P

BLK = 128
CAP = 2


def shards(tokens, route, blocks, weight, enc_bias, dec_bias):
    n_expert = lax.axis_size("expert")
    n_latent = lax.axis_size("latent")
    width = tokens.shape[1]
    list_len = blocks.shape[1]
    expert_of = route[:, 0]
    one_hot = (expert_of[:, None] == jnp.arange(n_expert, dtype=jnp.int32)[None, :]).astype(
        jnp.int32
    )
    earlier = jnp.sum((jnp.cumsum(one_hot, axis=0) - one_hot) * one_hot, axis=1)
    target = expert_of * CAP + earlier
    send_rows = jnp.zeros((n_expert * CAP, width), jnp.bfloat16).at[target].set(tokens)
    send_rows = send_rows.reshape(n_expert, CAP, width)
    send_lists = jnp.full((n_expert * CAP, list_len), -1, jnp.int32).at[target].set(blocks)
    send_lists = send_lists.reshape(n_expert, CAP, list_len)
    got_rows, got_lists = (
        lax.all_to_all(send_rows, "expert", split_axis=0, concat_axis=0, tiled=True),
        lax.all_to_all(send_lists, "expert", split_axis=0, concat_axis=0, tiled=True),
    )
    all_rows, all_lists = (
        lax.all_gather(got_rows[None], "latent", axis=0, tiled=True),
        lax.all_gather(got_lists[None], "latent", axis=0, tiled=True),
    )
    token_rows = all_rows.reshape(-1, width)
    listed = all_lists.reshape(-1, list_len)
    row_count = token_rows.shape[0]
    valid = (listed[:, 0] >= 0).astype(jnp.float32)
    slice_index = lax.axis_index("latent")
    weights_here = weight[0]
    per_slice = weights_here.shape[1] // BLK
    own_blocks = slice_index * per_slice + jnp.arange(per_slice, dtype=jnp.int32)
    chosen = jnp.any(listed[:, :, None] == own_blocks[None, None, :], axis=1).astype(jnp.float32)
    mask = jnp.repeat(chosen, BLK, axis=1)
    rows_f32 = token_rows.astype(jnp.float32)
    shifted = (rows_f32 - dec_bias).astype(jnp.bfloat16)
    pre_act = jnp.dot(shifted, weights_here, preferred_element_type=jnp.float32) + enc_bias[0]
    active = jnp.maximum(pre_act, 0.0) * mask
    active_bf = active.astype(jnp.bfloat16)
    share = row_count // n_latent
    first_row = slice_index * share
    along_width = (((1,), (1,)), ((), ()))
    partial_sum = lax.dot_general(
        active_bf, weights_here, along_width, preferred_element_type=jnp.float32
    )
    summed = lax.psum(partial_sum, "latent")
    error_all = (summed + dec_bias - rows_f32) * valid[:, None]
    error_bf = error_all.astype(jnp.bfloat16)
    error_share = lax.dynamic_slice_in_dim(error_all, first_row, share, 0)
    grad_act = jnp.dot(error_bf, weights_here, preferred_element_type=jnp.float32)
    grad_pre = grad_act * (pre_act > 0.0).astype(jnp.float32) * mask
    grad_pre_bf = grad_pre.astype(jnp.bfloat16)
    along_rows = (((0,), (0,)), ((), ()))
    grad_here = lax.dot_general(
        shifted, grad_pre_bf, along_rows, preferred_element_type=jnp.float32
    )
    grad_here = grad_here + lax.dot_general(
        error_bf, active_bf, along_rows, preferred_element_type=jnp.float32
    )
    grad_bias = jnp.sum(grad_pre, axis=0)
    pulled = jnp.dot(
        weights_here, grad_bias.astype(jnp.bfloat16), preferred_element_type=jnp.float32
    )
    bias_term = jnp.sum(error_share, axis=0) - pulled
    loss_term = 0.5 * jnp.sum(error_share * error_share)
    grad_dec, loss_sum = lax.psum((bias_term, loss_term), ("expert", "latent"))
    loss = loss_sum / (tokens.shape[0] * n_expert * n_latent)
    return (grad_here.astype(jnp.bfloat16)[None], grad_bias[None], grad_dec, loss)


def solution(mesh):
    return jax.shard_map(
        shards,
        mesh=mesh,
        in_specs=(
            P(("expert", "latent"), None),
            P(("expert", "latent"), None),
            P(("expert", "latent"), None),
            P("expert", None, "latent"),
            P("expert", "latent"),
            P(),
        ),
        out_specs=(P("expert", None, "latent"), P("expert", "latent"), P(), P()),
        check_vma=False,
    )
```

profile of v0, /device:TPU:1, one launch (start us, length us, event | category | flops | bytes accessed | tf_op | source)
XLA Modules:
  0.0 402.3 jit_solution(3232776257881222928)
XLA Ops:
  7.2 0.0 copy-start.4
  7.2 0.0 all-gather.4.cloned.1.call-start
  7.2 0.7 fusion.24
  8.0 0.8 select_reduce_fusion
  8.8 0.7 fusion.25
  9.5 0.9 scatter_custom_fusion
  10.4 11.2 %all_to_all.10 = bf16[8,2,2560]{2,1,0:T(2,128)(2,1)} all-to-all(bf16[8,2,2560]{2,1,0:T(2,128)(2,1)S(1)} %reshape.33), channel_id=1, replica_groups=mesh['expert'=8,'latent'=32] {'expert'}, dimensions={0} | all-to-all | bytes 163840 | tf_op jit(solution)/shard_map/all_to_all | solution.py:26
  21.6 0.0 all-gather.4.cloned.1.call-update
  21.7 0.8 scatter_custom_fusion.1
  22.4 0.7 reshape.68
  23.1 4.0 all-to-all-start.1
  27.1 0.0 all-reduce.3.cloned.1.call-start
  27.1 4.5 %all-to-all-done.1 = s32[8,1,128]{2,1,0:T(1,128)S(1)} async-done(((s32[8,1,128]{2,1,0:T(1,128)}), s32[8,1,128]{2,1,0:T(1,128)S(1)}, u32[]{:S(2)}, u32[]{:S(2)}) %all-to-all-start.1) | async-done | bytes 4128 | tf_op jit(solution)/shard_map/all_to_all | solution.py:27
  31.6 0.5 broadcast.43
  32.2 0.7 reduce.4
  32.8 0.1 reshape.69
  32.9 40.8 %all-gather.1 = s32[256,2,64]{2,1,0:T(2,128)S(1)} all-gather(s32[8,2,64]{2,1,0:T(2,128)S(1)} %reshape.69), channel_id=3, replica_groups=mesh['expert'=8,'latent'=32] {'latent'}, dimensions={0}, use_global_device_ids=true | all-gather | bytes 135168 | tf_op jit(solution)/shard_map/all_gather | solution.py:31
  73.7 0.1 copy.12
  73.8 0.2 compare_reduce_fusion
  74.1 0.1 copy.13
  74.2 24.0 %all-gather.4.cloned.1.call-done = bf16[256,2,2560]{2,1,0:T(2,128)(2,1)} async-done(((bf16[8,2,2560]{2,1,0:T(2,128)(2,1)}), bf16[256,2,2560]{2,1,0:T(2,128)(2,1)}) %all-gather.4.cloned.1.call-update) | async-done | bytes 2621456 | tf_op jit(solution)/shard_map/all_gather | solution.py:30
  98.1 3.5 convert_element_type.56
  101.7 0.0 copy-done.4
  101.7 2.3 subtract_convert_fusion
  104.0 0.0 copy-start.6
  104.0 2.6 convert_element_type.47
  106.6 0.0 slice-start.2
  106.6 0.6 broadcast_in_dim.32
  107.2 0.0 copy-start.1
  107.2 0.0 copy-done.6
  107.2 0.0 slice-start.3
  107.3 8.7 %fusion.11 = (bf16[512,1024]{1,0:T(8,128)(2,1)S(1)}, f32[512,1024]{1,0:T(8,128)}) fusion(f32[64,8,8,128]{3,2,1,0:T(8,128)S(1)} %bitcast.51, f32[1024]{0:T(1024)S(1)} %bitcast.57, bf16[512,2560]{1,0:T(8,128)(2,1)} %convert_element_type.47, bf16[1,2560,1024]{2,1,0:T(8,128)(2,1)} %param.9), kind=kOutput, calls=%fused_computation.19 | convolution fusion | flops 2686451712 | bytes 13111296 | tf_op jit(solution)/shard_map/dot_general | solution.py:45
  116.0 0.0 copy-done.1
  116.0 0.0 copy-start.3
  116.0 1.0 copy-done.3
  117.0 0.0 slice-done.2
  117.0 0.0 slice-done.3
  117.0 4.7 %fusion.4 = f32[512,2560]{1,0:T(8,128)} fusion(bf16[512,1024]{1,0:T(8,128)(2,1)S(1)} %get-tuple-element.8, bf16[1,2560,1024]{2,1,0:T(8,128)(2,1)S(1)} %bitcast.46), kind=kOutput, calls=%fused_computation.7 | convolution fusion | flops 2684354560 | bytes 11534336 | tf_op jit(solution)/shard_map/dot_general | solution.py:51
  121.7 0.0 copy-start
  121.7 0.0 all-reduce.3.cloned.1.call-update
  121.7 0.1 convert_reduce_fusion
  121.8 1.6 copy-done
  123.4 2.9 reshape.36
  126.3 0.0 copy-start.2
  126.4 168.2 %all-reduce.3.cloned.1.call-done = f32[512,2560]{1,0:T(8,128)} async-done(((f32[512,2560]{1,0:T(8,128)}), f32[512,2560]{1,0:T(8,128)}) %all-reduce.3.cloned.1.call-update) | async-done | bytes 5242896 | tf_op jit(solution)/shard_map/psum | solution.py:54
  294.5 0.0 copy-start.7
  294.5 4.9 %subtract_multiply_fusion = f32[512,2560]{1,0:T(8,128)S(1)} fusion(f32[512,2560]{1,0:T(8,128)} %reshape.36, f32[512,2560]{1,0:T(8,128)} %all-reduce.3.cloned.1.call-done, f32[512]{0:T(512)S(1)} %convert_reduce_fusion, f32[2560]{0:T(1024)S(1)} %copy-done.4), kind=kLoop, calls=%fused_computation.11 | loop fusion | flops 3932160 | bytes 15740928 | tf_op jit(solution)/shard_map/mul | solution.py:55
  299.4 0.0 copy-done.2
  299.5 0.0 copy-done.7
  299.5 0.0 slice-start.1
  299.5 5.9 %fusion.26 = (f32[1024]{0:T(1024)S(1)}, bf16[512,1024]{1,0:T(8,128)(2,1)S(1)}) fusion(f32[64,8,8,128]{3,2,1,0:T(8,128)S(1)} %bitcast.52, bf16[1,2560,1024]{2,1,0:T(8,128)(2,1)} %param.9, f32[512,2560]{1,0:T(8,128)S(1)} %subtract_multiply_fusion, f32[512,1024]{1,0:T(8,128)S(1)} %copy-done.7, f32[1024]{0:T(1024)S(1)} %bitcast.58), kind=kOutput, calls=%fused_computation.40 | convolution fusion | flops 2688809984 | bytes 15736832 | tf_op jit(solution)/shard_map/dot_general | solution.py:58
  305.4 0.0 copy-start.5
  305.4 0.0 slice-done
  305.4 0.0 slice-done.1
  305.4 0.0 slice-start.4
  305.5 3.0 fusion.9
  308.5 0.0 slice-start.5
  308.5 6.5 %fusion.8 = bf16[1,2560,1024]{2,1,0:T(8,128)(2,1)} fusion(f32[2560,1024]{1,0:T(8,128)S(1)} %fusion.9, bf16[512,1024]{1,0:T(8,128)(2,1)} %copy-done.3, f32[512,2560]{1,0:T(8,128)S(1)} %subtract_multiply_fusion), kind=kOutput, calls=%fused_computation.14 | convolution fusion | flops 2690908160 | bytes 22020096 | tf_op jit(solution)/shard_map/dot_general | solution.py:65
  315.0 0.6 multiply_reduce_fusion
  315.6 0.0 copy-done.5
  315.6 0.0 slice-done.4
  315.6 0.0 slice-done.5
  315.6 1.5 fusion.16
  317.8 75.9 %all-reduce = (f32[2560]{0:T(1024)}, f32[]{:T(128)}) all-reduce(f32[2560]{0:T(1024)S(1)} %sub.28, f32[]{:T(128)S(6)} %mul_shard_map.3), channel_id=1, replica_groups=mesh['expert'=8,'latent'=32] {'expert','latent'}, use_global_device_ids=true, to_apply=%region_8.9 | all-reduce | flops 2561 | bytes 20488 | tf_op jit(solution)/shard_map/psum | solution.py:74
  (11 shorter events, 0.1 us)
Async XLA Ops:
  7.2 94.5 %copy-start.4 = (f32[2560]{0:T(1024)S(1)}, f32[2560]{0:T(1024)}, u32[]{:S(2)}) copy-start(f32[2560]{0:T(1024)} %param.11) | copy-start | bytes 30724
  7.2 91.0 %all-gather.4.cloned.1.call-start = ((), (), s32[]{:S(2)}) async-start(), calls=%async_computation.3 | async-start | bytes 2703360 | tf_op jit(solution)/shard_map/all_gather | solution.py:30
  23.1 8.5 %all-to-all-start.1 = ((s32[8,1,128]{2,1,0:T(1,128)}), s32[8,1,128]{2,1,0:T(1,128)S(1)}, u32[]{:S(2)}, u32[]{:S(2)}) async-start(s32[8,1,128]{2,1,0:T(1,128)} %reshape.68), calls=%async_computation.1 | async-start | bytes 8192 | tf_op jit(solution)/shard_map/all_to_all | solution.py:27
  27.1 267.4 %all-reduce.3.cloned.1.call-start = ((), (), s32[]{:S(2)}) async-start(), calls=%async_computation.2 | async-start | bytes 10485760 | tf_op jit(solution)/shard_map/psum | solution.py:54
  104.0 3.2 copy-start.6
  106.6 10.4 %slice-start.2 = ((s8[5242880]{0:T(1024)(128)(4,1)}), s8[4194304]{0:T(1024)(128)(4,1)S(1)}, s32[]{:S(2)}) async-start(s8[5242880]{0:T(1024)(128)(4,1)} %bitcast.45), calls=%async_computation.6 | async-start | bytes 8388608
  107.2 8.8 %copy-start.1 = (f32[512,8,128]{2,1,0:T(8,128)}, f32[512,8,128]{2,1,0:T(8,128)S(1)}, u32[]{:S(2)}) copy-start(f32[512,8,128]{2,1,0:T(8,128)S(1)} %broadcast_in_dim.32) | copy-start | bytes 6291460
  107.2 9.7 %slice-start.3 = ((s8[5242880]{0:T(1024)(128)(4,1)}), s8[1048576]{0:T(1024)(128)(4,1)S(1)}, s32[]{:S(2)}) async-start(s8[5242880]{0:T(1024)(128)(4,1)} %bitcast.45), calls=%async_computation.7 | async-start | bytes 2097152
  116.0 1.0 copy-start.3
  121.7 1.7 copy-start
  126.3 173.1 %copy-start.2 = (f32[512,8,128]{2,1,0:T(8,128)S(1)}, f32[512,8,128]{2,1,0:T(8,128)}, u32[]{:S(2)}) copy-start(f32[512,8,128]{2,1,0:T(8,128)} %copy-done.1) | copy-start | bytes 6291460
  294.5 4.9 %copy-start.7 = (f32[512,1024]{1,0:T(8,128)S(1)}, f32[512,1024]{1,0:T(8,128)}, u32[]{:S(2)}) copy-start(f32[512,1024]{1,0:T(8,128)} %get-tuple-element.9) | copy-start | bytes 6291460
  294.5 10.9 %slice-start = ((s8[5242880]{0:T(1024)(128)(4,1)}), s8[1048576]{0:T(1024)(128)(4,1)S(1)}, s32[]{:S(2)}) async-start(s8[5242880]{0:T(1024)(128)(4,1)} %bitcast.42), calls=%async_computation.4 | async-start | bytes 2097152
  299.5 6.0 %slice-start.1 = ((s8[5242880]{0:T(1024)(128)(4,1)}), s8[4194304]{0:T(1024)(128)(4,1)S(1)}, s32[]{:S(2)}) async-start(s8[5242880]{0:T(1024)(128)(4,1)} %bitcast.42), calls=%async_computation.5 | async-start | bytes 8388608
  305.4 10.2 %copy-start.5 = (f32[1024]{0:T(1024)}, f32[1024]{0:T(1024)S(1)}, u32[]{:S(2)}) copy-start(f32[1024]{0:T(1024)S(1)} %get-tuple-element.10) | copy-start | bytes 12292
  305.4 10.2 %slice-start.4 = ((s8[5242880]{0:T(1024)(128)(4,1)}), s8[4194304]{0:T(1024)(128)(4,1)S(1)}, s32[]{:S(2)}) async-start(s8[5242880]{0:T(1024)(128)(4,1)} %bitcast.47), calls=%async_computation.8 | async-start | bytes 8388608
  308.5 7.2 %slice-start.5 = ((s8[5242880]{0:T(1024)(128)(4,1)}), s8[1048576]{0:T(1024)(128)(4,1)S(1)}, s32[]{:S(2)}) async-start(s8[5242880]{0:T(1024)(128)(4,1)} %bitcast.47), calls=%async_computation.9 | async-start | bytes 2097152
Sparse Core Ops, SparseCore 0:
  21.8 76.3 all-gather.3
  121.8 172.6 all-reduce.2
where the time goes:
time: 403 us; the launch traced here: 402 us
  waiting for transfers between devices  197 us (49%)
  blocking collectives  128 us (32%)
  matrix products  30.3 us (8%)
  between operations  16.7 us (4%)
  other arithmetic  14.6 us (4%)
  local copies, waits for them, and re-layouts  12 us (3%)
  starting transfers between devices  4.05 us (1%)
    psum x1, waiting for transfers between devices, shards(): summed = lax.psum(partial_sum, 'latent')  168 us
    psum x1, blocking collectives, shards(): grad_dec, loss_sum = lax.psum((bias_term, loss_term), ('expert', 'latent'))  75.9 us
    all_gather x1, blocking collectives, shards(): lax.all_gather(got_lists[None], 'latent', axis=0, tiled=True)  40.8 us
    all_gather x1, waiting for transfers between devices, shards(): lax.all_gather(got_rows[None], 'latent', axis=0, tiled=True)  24 us
    all_to_all x1, blocking collectives, shards(): lax.all_to_all(send_rows, 'expert', split_axis=0, concat_axis=0, tiled=True)  11.2 us
    dot_general x1, matrix products, shards(): jnp.dot(shifted, weights_here, preferred_element_type=jnp.float32)  8.73 us
  transfers between devices with their start and end apart: 3, of which 3 were waited for; matrix products, arithmetic and copies ran while one was open for 2% of the time, Pallas kernels for 0%

commit v1 on v0

--- a/solution.py
+++ b/solution.py
@@ -26,8 +26,11 @@
         lax.all_to_all(send_rows, "expert", split_axis=0, concat_axis=0, tiled=True),
         lax.all_to_all(send_lists, "expert", split_axis=0, concat_axis=0, tiled=True),
     )
+    indices_group = lambda v0: jnp.concatenate(
+        lax.all_to_all(jnp.stack(lax.axis_size("latent") * [v0]), "latent", 0, 0), axis=0
+    )
     all_rows, all_lists = (
-        lax.all_gather(got_rows[None], "latent", axis=0, tiled=True),
+        indices_group(got_rows[None]),
         lax.all_gather(got_lists[None], "latent", axis=0, tiled=True),
     )
     token_rows = all_rows.reshape(-1, width)

time: 403 us -> 449 us (1.11)
  blocking collectives: 128 us -> 172 us
  waiting for transfers between devices: 197 us -> 181 us
  starting transfers between devices: 4.05 us -> 17 us
  local copies, waits for them, and re-layouts: 12 us -> 18.3 us
    all_gather x1, blocking collectives: 40.8 us -> 88.5 us  [shards(): lax.all_gather(got_lists[None], 'latent', axis=0, tiled=True)]
    all_gather x1 -> x0, waiting for transfers between devices: 24 us -> none  [shards(): lax.all_gather(got_rows[None], 'latent', axis=0, tiled=True)]
    all_to_all x0 -> x1, starting transfers between devices: none -> 10.5 us  [shards(): lax.all_to_all(jnp.stack(lax.axis_size('latent') * [v0]), 'latent', 0, 0)]
    psum x1, waiting for transfers between devices: 168 us -> 177 us  [shards(): summed = lax.psum(partial_sum, 'latent')]
  transfers between devices with their start and end apart: 3 -> 3, of which waited for: 3 -> 2; matrix products, arithmetic and copies ran while one was open for 2% -> 1% of each run, Pallas kernels for 0% -> 0%
where the time goes in v1:
time: 449 us
  waiting for transfers between devices  181 us (40%)
  blocking collectives  172 us (38%)
  matrix products  30.3 us (7%)
  local copies, waits for them, and re-layouts  18.3 us (4%)
  starting transfers between devices  17 us (4%)
  between operations  16.7 us (4%)
  other arithmetic  13.1 us (3%)
    psum x1, waiting for transfers between devices, shards(): summed = lax.psum(partial_sum, 'latent')  177 us
    all_gather x1, blocking collectives, shards(): lax.all_gather(got_lists[None], 'latent', axis=0, tiled=True)  88.5 us
    psum x1, blocking collectives, shards(): grad_dec, loss_sum = lax.psum((bias_term, loss_term), ('expert', 'latent'))  75.9 us
    all_to_all x1, starting transfers between devices, shards(): lax.all_to_all(jnp.stack(lax.axis_size('latent') * [v0]), 'latent', 0, 0)  10.5 us
  transfers between devices with their start and end apart: 3, of which 2 were waited for; matrix products, arithmetic and copies ran while one was open for 1% of the time, Pallas kernels for 0%

profile of v1, /device:TPU:1, one launch (start us, length us, event | category | flops | bytes accessed | tf_op | source)
XLA Modules:
  0.0 448.6 jit_solution(16160862069241635782)
XLA Ops:
  7.2 0.0 copy-start.3
  7.2 0.7 fusion.24
  7.9 0.8 select_reduce_fusion
  8.8 0.7 fusion.25
  9.4 0.8 scatter_custom_fusion.1
  10.2 0.7 reshape.65
  10.9 6.5 %all-to-all-start.2 = ((s32[8,1,128]{2,1,0:T(1,128)}), s32[8,1,128]{2,1,0:T(1,128)S(1)}, u32[]{:S(2)}, u32[]{:S(2)}) async-start(s32[8,1,128]{2,1,0:T(1,128)} %reshape.65), calls=%async_computation.2 | async-start | bytes 8192 | tf_op jit(solution)/shard_map/all_to_all | solution.py:27
  17.3 0.9 scatter_custom_fusion
  18.3 3.6 all-to-all-done.2
  21.8 8.0 %all_to_all.15 = bf16[8,2,2560]{2,1,0:T(2,128)(2,1)S(1)} all-to-all(bf16[8,2,2560]{2,1,0:T(2,128)(2,1)S(1)} %reshape.34), channel_id=1, replica_groups=mesh['expert'=8,'latent'=32] {'expert'}, dimensions={0} | all-to-all | bytes 163840 | tf_op jit(solution)/shard_map/all_to_all | solution.py:26
  29.8 3.9 stack.3
  33.7 10.5 %all-to-all-start.1 = ((bf16[32,1,8,2,2560]{4,3,2,1,0:T(2,128)(2,1)}), bf16[32,1,8,2,2560]{4,3,2,1,0:T(2,128)(2,1)S(1)}, u32[]{:S(2)}, u32[]{:S(2)}) async-start(bf16[32,1,8,2,2560]{4,3,2,1,0:T(2,128)(2,1)} %stack.3), calls=%async_computation.1 | async-start | bytes 5242880 | tf_op jit(solution)/shard_map/all_to_all | solution.py:30
  44.2 0.0 all-reduce.3.cloned.1.call-start
  44.3 0.5 broadcast.45
  44.8 0.7 reduce.4
  45.5 0.1 reshape.66
  45.5 88.5 %all-gather = s32[256,2,64]{2,1,0:T(2,128)S(1)} all-gather(s32[8,2,64]{2,1,0:T(2,128)S(1)} %reshape.66), channel_id=2, replica_groups=mesh['expert'=8,'latent'=32] {'latent'}, dimensions={0}, use_global_device_ids=true | all-gather | bytes 135168 | tf_op jit(solution)/shard_map/all_gather | solution.py:34
  134.0 0.1 copy.12
  134.1 0.2 compare_reduce_fusion
  134.4 0.1 copy.13
  134.5 0.0 copy-start.5
  134.5 0.0 all-to-all-done.1
  134.5 0.0 copy-done.3
  134.5 4.3 subtract_convert_fusion
  138.8 6.7 %convert_element_type.47 = bf16[512,2560]{1,0:T(8,128)(2,1)} reshape(bf16[32,1,8,2,2560]{4,3,2,1,0:T(2,128)(2,1)} %subtract_convert_fusion) | data formatting | bytes 5242880 | tf_op jit(solution)/shard_map/convert_element_type | solution.py:47
  145.5 0.0 slice-start.2
  145.5 0.6 broadcast_in_dim.28
  146.1 0.0 copy-start
  146.1 0.0 copy-done.5
  146.1 0.0 slice-start.3
  146.1 8.8 %fusion.11 = (bf16[512,1024]{1,0:T(8,128)(2,1)S(1)}, f32[512,1024]{1,0:T(8,128)}) fusion(f32[64,8,8,128]{3,2,1,0:T(8,128)S(1)} %bitcast.49, f32[1024]{0:T(1024)S(1)} %bitcast.55, bf16[512,2560]{1,0:T(8,128)(2,1)} %convert_element_type.47, bf16[1,2560,1024]{2,1,0:T(8,128)(2,1)} %param.9), kind=kOutput, calls=%fused_computation.19 | convolution fusion | flops 2686451712 | bytes 13111296 | tf_op jit(solution)/shard_map/dot_general | solution.py:48
  154.9 0.0 copy-done
  154.9 0.0 copy-start.2
  154.9 1.0 copy-done.2
  155.9 0.0 slice-done.2
  155.9 0.0 slice-done.3
  155.9 4.7 %fusion.4 = f32[512,2560]{1,0:T(8,128)} fusion(bf16[512,1024]{1,0:T(8,128)(2,1)S(1)} %get-tuple-element.8, bf16[1,2560,1024]{2,1,0:T(8,128)(2,1)S(1)} %bitcast.44), kind=kOutput, calls=%fused_computation.7 | convolution fusion | flops 2684354560 | bytes 11534336 | tf_op jit(solution)/shard_map/dot_general | solution.py:54
  160.6 0.0 all-reduce.3.cloned.1.call-update
  160.6 0.1 convert_reduce_fusion
  160.8 2.9 reshape.37
  163.7 0.0 copy-start.1
  163.7 177.3 %all-reduce.3.cloned.1.call-done = f32[512,2560]{1,0:T(8,128)} async-done(((f32[512,2560]{1,0:T(8,128)}), f32[512,2560]{1,0:T(8,128)}) %all-reduce.3.cloned.1.call-update) | async-done | bytes 5242896 | tf_op jit(solution)/shard_map/psum | solution.py:57
  341.0 0.0 copy-start.6
  341.0 0.0 slice-start
  341.0 4.9 %subtract_multiply_fusion = f32[512,2560]{1,0:T(8,128)S(1)} fusion(f32[512,2560]{1,0:T(8,128)} %reshape.37, f32[512,2560]{1,0:T(8,128)} %all-reduce.3.cloned.1.call-done, f32[512]{0:T(512)S(1)} %convert_reduce_fusion, f32[2560]{0:T(1024)S(1)} %copy-done.3), kind=kLoop, calls=%fused_computation.11 | loop fusion | flops 3932160 | bytes 15740928 | tf_op jit(solution)/shard_map/mul | solution.py:58
  345.8 0.0 copy-done.1
  345.8 0.0 copy-done.6
  345.9 0.0 slice-start.1
  345.9 5.9 %fusion.26 = (f32[1024]{0:T(1024)S(1)}, bf16[512,1024]{1,0:T(8,128)(2,1)S(1)}) fusion(f32[64,8,8,128]{3,2,1,0:T(8,128)S(1)} %bitcast.50, bf16[1,2560,1024]{2,1,0:T(8,128)(2,1)} %param.9, f32[512,2560]{1,0:T(8,128)S(1)} %subtract_multiply_fusion, f32[512,1024]{1,0:T(8,128)S(1)} %copy-done.6, f32[1024]{0:T(1024)S(1)} %bitcast.56), kind=kOutput, calls=%fused_computation.40 | convolution fusion | flops 2688809984 | bytes 15736832 | tf_op jit(solution)/shard_map/dot_general | solution.py:61
  351.8 0.0 copy-start.4
  351.8 0.0 slice-done
  351.8 0.0 slice-done.1
  351.8 0.0 slice-start.4
  351.8 3.0 fusion.9
  354.8 0.0 slice-start.5
  354.8 6.5 %fusion.8 = bf16[1,2560,1024]{2,1,0:T(8,128)(2,1)} fusion(f32[2560,1024]{1,0:T(8,128)S(1)} %fusion.9, bf16[512,1024]{1,0:T(8,128)(2,1)} %copy-done.2, f32[512,2560]{1,0:T(8,128)S(1)} %subtract_multiply_fusion), kind=kOutput, calls=%fused_computation.14 | convolution fusion | flops 2690908160 | bytes 22020096 | tf_op jit(solution)/shard_map/dot_general | solution.py:68
  361.3 0.6 multiply_reduce_fusion
  362.0 0.0 copy-done.4
  362.0 0.0 slice-done.4
  362.0 0.0 slice-done.5
  362.0 1.5 fusion.16
  364.1 75.9 %all-reduce = (f32[2560]{0:T(1024)}, f32[]{:T(128)}) all-reduce(f32[2560]{0:T(1024)S(1)} %sub.28, f32[]{:T(128)S(6)} %mul_shard_map.3), channel_id=1, replica_groups=mesh['expert'=8,'latent'=32] {'expert','latent'}, use_global_device_ids=true, to_apply=%region_8.9 | all-reduce | flops 2561 | bytes 20488 | tf_op jit(solution)/shard_map/psum | solution.py:77
  (10 shorter events, 0.1 us)
Async XLA Ops:
  7.2 127.3 %copy-start.3 = (f32[2560]{0:T(1024)S(1)}, f32[2560]{0:T(1024)}, u32[]{:S(2)}) copy-start(f32[2560]{0:T(1024)} %param.11) | copy-start | bytes 30724
  10.9 11.0 %all-to-all-start.2 = ((s32[8,1,128]{2,1,0:T(1,128)}), s32[8,1,128]{2,1,0:T(1,128)S(1)}, u32[]{:S(2)}, u32[]{:S(2)}) async-start(s32[8,1,128]{2,1,0:T(1,128)} %reshape.65), calls=%async_computation.2 | async-start | bytes 8192 | tf_op jit(solution)/shard_map/all_to_all | solution.py:27
  33.7 100.8 %all-to-all-start.1 = ((bf16[32,1,8,2,2560]{4,3,2,1,0:T(2,128)(2,1)}), bf16[32,1,8,2,2560]{4,3,2,1,0:T(2,128)(2,1)S(1)}, u32[]{:S(2)}, u32[]{:S(2)}) async-start(bf16[32,1,8,2,2560]{4,3,2,1,0:T(2,128)(2,1)} %stack.3), calls=%async_computation.1 | async-start | bytes 5242880 | tf_op jit(solution)/shard_map/all_to_all | solution.py:30
  44.2 296.8 %all-reduce.3.cloned.1.call-start = ((), (), s32[]{:S(2)}) async-start(), calls=%async_computation.3 | async-start | bytes 10485760 | tf_op jit(solution)/shard_map/psum | solution.py:57
  134.5 11.6 %copy-start.5 = (f32[1,1024]{1,0:T(1,128)S(1)}, f32[1,1024]{1,0:T(1,128)}, u32[]{:S(2)}) copy-start(f32[1,1024]{1,0:T(1,128)} %param.10) | copy-start | bytes 12292
  145.5 10.4 %slice-start.2 = ((s8[5242880]{0:T(1024)(128)(4,1)}), s8[4194304]{0:T(1024)(128)(4,1)S(1)}, s32[]{:S(2)}) async-start(s8[5242880]{0:T(1024)(128)(4,1)} %bitcast.43), calls=%async_computation.6 | async-start | bytes 8388608
  146.1 8.8 %copy-start = (f32[512,8,128]{2,1,0:T(8,128)}, f32[512,8,128]{2,1,0:T(8,128)S(1)}, u32[]{:S(2)}) copy-start(f32[512,8,128]{2,1,0:T(8,128)S(1)} %broadcast_in_dim.28) | copy-start | bytes 6291460
  146.1 9.8 %slice-start.3 = ((s8[5242880]{0:T(1024)(128)(4,1)}), s8[1048576]{0:T(1024)(128)(4,1)S(1)}, s32[]{:S(2)}) async-start(s8[5242880]{0:T(1024)(128)(4,1)} %bitcast.43), calls=%async_computation.7 | async-start | bytes 2097152
  154.9 1.0 copy-start.2
  163.7 182.1 %copy-start.1 = (f32[512,8,128]{2,1,0:T(8,128)S(1)}, f32[512,8,128]{2,1,0:T(8,128)}, u32[]{:S(2)}) copy-start(f32[512,8,128]{2,1,0:T(8,128)} %copy-done) | copy-start | bytes 6291460
  341.0 4.9 %copy-start.6 = (f32[512,1024]{1,0:T(8,128)S(1)}, f32[512,1024]{1,0:T(8,128)}, u32[]{:S(2)}) copy-start(f32[512,1024]{1,0:T(8,128)} %get-tuple-element.9) | copy-start | bytes 6291460
  341.0 10.8 %slice-start = ((s8[5242880]{0:T(1024)(128)(4,1)}), s8[1048576]{0:T(1024)(128)(4,1)S(1)}, s32[]{:S(2)}) async-start(s8[5242880]{0:T(1024)(128)(4,1)} %bitcast.41), calls=%async_computation.4 | async-start | bytes 2097152
  345.9 6.0 %slice-start.1 = ((s8[5242880]{0:T(1024)(128)(4,1)}), s8[4194304]{0:T(1024)(128)(4,1)S(1)}, s32[]{:S(2)}) async-start(s8[5242880]{0:T(1024)(128)(4,1)} %bitcast.41), calls=%async_computation.5 | async-start | bytes 8388608
  351.8 10.2 %copy-start.4 = (f32[1024]{0:T(1024)}, f32[1024]{0:T(1024)S(1)}, u32[]{:S(2)}) copy-start(f32[1024]{0:T(1024)S(1)} %get-tuple-element.10) | copy-start | bytes 12292
  351.8 10.2 %slice-start.4 = ((s8[5242880]{0:T(1024)(128)(4,1)}), s8[4194304]{0:T(1024)(128)(4,1)S(1)}, s32[]{:S(2)}) async-start(s8[5242880]{0:T(1024)(128)(4,1)} %bitcast.45), calls=%async_computation.8 | async-start | bytes 8388608
  354.8 7.2 %slice-start.5 = ((s8[5242880]{0:T(1024)(128)(4,1)}), s8[1048576]{0:T(1024)(128)(4,1)S(1)}, s32[]{:S(2)}) async-start(s8[5242880]{0:T(1024)(128)(4,1)} %bitcast.45), calls=%async_computation.9 | async-start | bytes 2097152
Sparse Core Ops, SparseCore 0:
  160.8 180.1 all-reduce.2
